TPU v7x, 32 devices: a whole 2x2x4 slice. The times are simulated.
32 devices in a mesh: shot: 2 (over y), box: 8 (over z, x), sub: 2 (over core).
Axes of the slice: x: 2, y: 2, z: 4, core: 2. Of those that a mesh axis runs over, the one named last changes fastest.
Arguments:
- box_weights: float32 [64, 256, 128], P(('shot', 'box', 'sub')), parts along dimension 0, may hold values from -6 to 6
- velocity: float32 [8192], P('shot'), parts along dimension 0, may hold values from -4 to 4
- switch_kernel: float32 [128, 128], replicated, may hold values from -0.5 to 0.5
Outputs:
- final_weights: float32 [4, 4096, 128], P('shot', ('box', 'sub')), parts along dimension 0
There are 2 independent parts, one for each index of `shot`. A program takes and returns all parts, laid end to end along the dimension named above; an argument that names none is the same for every part. Nothing has to cross between parts.
All inputs are finite; a program needn't handle non-finite values.
Results may differ from a plain program's by a relative error of at most 0.00013.
Values sent between devices are 32-bit elements; how exact they have to be, the bound alone decides.
No kernel may reach another device: no remote copies, remote signals or barrier semaphores. Data moves between devices by JAX's collectives and lax.ppermute only.
A program may use at most 64 MiB of HBM per device.

v0:
```python
import jax
import jax.numpy as jnp
from jax import lax
from jax.sharding import PartitionSpec as P

CHEB = 8
half_root = 0.7071067811865476


def swapped(value, axis, apart):
    mask = 2**apart
    pairs = [(source, source ^ mask) for source in range(lax.axis_size(axis))]
    return lax.ppermute(value, axis, pairs)


def cheb_nodes():
    counter = jnp.arange(CHEB, dtype=jnp.float32)
    return jnp.cos(jnp.pi * (2.0 * counter + 1.0) / (2.0 * CHEB))


def lagrange_rows(points, node_values):
    differences = points[:, None] - node_values[None, :]
    node_gaps = node_values[:, None] - node_values[None, :]
    identity = jnp.eye(CHEB, dtype=jnp.float32)
    numerator = jnp.prod(
        jnp.where(identity[None, :, :] > 0.5, 1.0, differences[:, None, :]), axis=2
    )
    denominator = jnp.prod(jnp.where(identity > 0.5, 1.0, node_gaps), axis=1)
    return numerator / denominator[None, :]


def spread_coord(values, axis_dim):
    if axis_dim == 0:
        return jnp.repeat(values, CHEB)
    return jnp.tile(values, CHEB)


def level_tables(axis_dim):
    node_values = cheb_nodes()
    identity = jnp.eye(CHEB, dtype=jnp.float32)
    pair_eye = jnp.eye(2, dtype=jnp.float32)
    matrices = []
    coords = []
    for child_idx in (0, 1):
        child_pts = (node_values + (2.0 * child_idx - 1.0)) * 0.5
        lagrange = lagrange_rows(child_pts, node_values)
        if axis_dim == 0:
            single = jnp.kron(lagrange, identity)
        else:
            single = jnp.kron(identity, lagrange)
        matrices.append(jnp.kron(pair_eye, single))
        coords.append(spread_coord(child_pts, axis_dim))
    return (jnp.concatenate(matrices, 0), jnp.stack(coords), spread_coord(node_values, axis_dim))


def rotate(values, angles):
    real_part = values[..., : CHEB * CHEB]
    imag_part = values[..., CHEB * CHEB :]
    cosines = jnp.cos(angles)
    sine_vals = jnp.sin(angles)
    return jnp.concatenate(
        [real_part * cosines - imag_part * sine_vals, real_part * sine_vals + imag_part * cosines],
        -1,
    )


def merge_blocks(blocks, omegas, weights, coord_in, coord_out):
    phase = omegas[None, None, :, :, None]
    first_term = rotate(blocks[:, 0][:, :, None], -phase * coord_in[0])
    second_term = rotate(blocks[:, 1][:, :, None], -phase * coord_in[1])
    joined = jnp.concatenate([first_term, second_term], -1)
    mixture = jnp.dot(
        joined.reshape(-1, 4 * CHEB * CHEB),
        weights,
        precision=lax.Precision.HIGHEST,
        preferred_element_type=jnp.float32,
    )
    mixture = mixture.reshape(first_term.shape)
    return rotate(mixture, phase * coord_out) * half_root


def apply_switch(current, switch_kernel):
    flat = jnp.dot(
        current.reshape(-1, current.shape[-1]),
        switch_kernel,
        precision=lax.Precision.HIGHEST,
        preferred_element_type=jnp.float32,
    )
    return flat.reshape(current.shape)


def level_omegas(velocity, device, level_idx, tgt_count):
    tgt_code = device % 2 ** (level_idx + 1)
    return lax.dynamic_slice_in_dim(velocity, tgt_code * tgt_count, tgt_count)


def own_part(current, omegas, my_child, level_idx):
    vec_len = current.shape[-1]
    weights, coord_in, coord_out = level_tables(level_idx % 2)
    coord_mine = jnp.where(my_child == 0, coord_in[0], coord_in[1])
    weight_mine = jnp.where(my_child == 0, weights[:vec_len], weights[vec_len:])
    turned = rotate(current, -omegas[None, :, None] * coord_mine[None, None, :])
    return jnp.dot(
        turned.reshape(-1, vec_len),
        weight_mine,
        precision=lax.Precision.HIGHEST,
        preferred_element_type=jnp.float32,
    )


def far_part(own_term, partner, omegas, my_child, level_idx):
    vec_len = partner.shape[-1]
    weights, coord_in, coord_out = level_tables(level_idx % 2)
    coord_other = jnp.where(my_child == 0, coord_in[1], coord_in[0])
    weight_other = jnp.where(my_child == 0, weights[vec_len:], weights[:vec_len])
    turned = rotate(partner, -omegas[None, :, None] * coord_other[None, None, :])
    far_term = jnp.dot(
        turned.reshape(-1, vec_len),
        weight_other,
        precision=lax.Precision.HIGHEST,
        preferred_element_type=jnp.float32,
    )
    mixture = (own_term + far_term).reshape(partner.shape)
    return rotate(mixture, omegas[None, :, None] * coord_out[None, None, :]) * half_root


def body(box_weights, velocity, switch_kernel):
    box_count = lax.axis_size("box")
    sub_count = lax.axis_size("sub")
    box_bits = box_count.bit_length() - 1
    sub_bits = sub_count.bit_length() - 1
    levels = box_bits + sub_bits
    box_index = lax.axis_index("box")
    sub_index = lax.axis_index("sub")
    device = box_index * sub_count + sub_index
    src_count = box_weights.shape[0]
    tgt_count = box_weights.shape[1]
    vec_len = box_weights.shape[2]
    current = box_weights
    bit_idx = 0
    level_idx = bit_idx
    my_child = sub_index // 2**bit_idx % 2
    omegas = level_omegas(velocity, device, level_idx, tgt_count)
    own_term = own_part(current, omegas, my_child, level_idx)
    partner = swapped(current, "sub", bit_idx)
    current = far_part(own_term, partner, omegas, my_child, level_idx)
    spread = lax.all_to_all(current, "box", split_axis=1, concat_axis=0, tiled=True)
    block_width = tgt_count // box_count
    for bit_idx in range(box_bits):
        level_idx = sub_bits + bit_idx
        weights, coord_in, coord_out = level_tables(level_idx % 2)
        row_count = spread.shape[0]
        col_count = spread.shape[1]
        groups = 2 ** (bit_idx + 1)
        vel_table = velocity[: sub_count * groups * tgt_count].reshape(groups, sub_count, tgt_count)
        omegas = lax.dynamic_slice(
            vel_table, (0, sub_index, box_index * block_width), (groups, 1, block_width)
        )
        omegas = omegas.reshape(2, col_count)
        blocks = spread.reshape(row_count // (2 * src_count), 2, src_count, col_count, vec_len)
        merged = merge_blocks(blocks, omegas, weights, coord_in, coord_out)
        spread = merged.reshape(row_count // 2, 2 * col_count, vec_len)
        if level_idx == levels // 2 - 1:
            spread = apply_switch(spread, switch_kernel)
    current = lax.all_to_all(spread, "box", split_axis=1, concat_axis=1, tiled=True)
    return current


def solution(mesh):
    return jax.shard_map(
        body,
        mesh=mesh,
        in_specs=(P(("shot", "box", "sub"), None, None), P("shot"), P()),
        out_specs=P("shot", ("box", "sub"), None),
        check_vma=False,
    )
```

profile of v0, /device:TPU:0, one launch (start us, length us, event | category | flops | bytes accessed | tf_op | source)
XLA Modules:
  0.0 46.1 jit_solution(10633600639100690880)
XLA Ops:
  0.0 0.5 %collective-permute-start = (f32[2,256,128]{2,1,0:T(8,128)}, f32[2,256,128]{2,1,0:T(8,128)S(1)}, u32[]{:S(2)}, u32[]{:S(2)}) collective-permute-start(f32[2,256,128]{2,1,0:T(8,128)} %param.3), channel_id=1, source_target_pairs={{0,1},{1,0},{2,3},{3,2},{4,5},{5,4},{6,7},{7,6},{8,9},{9,8},{10,11... | collective-permute-start | bytes 786440 | tf_op jit(solution)/shard_map/ppermute | solution.py:13
  0.7 0.7 %copy-done.2 = f32[4096]{0:T(1024)S(1)} copy-done((f32[4096]{0:T(1024)S(1)}, f32[4096]{0:T(1024)}, u32[]{:S(2)}) %copy-start.2) | copy-done | bytes 16408
  1.8 0.2 select_reduce_fusion.2
  2.0 0.3 select_reduce_fusion.1
  2.3 0.1 broadcast_multiply_fusion
  2.5 0.1 mul.1285
  2.6 0.1 mul.1290
  2.8 0.1 mul.1344
  2.9 0.1 mul.1350
  3.2 0.5 %slice-done.1 = f32[2048]{0:T(1024)S(1)} async-done(((f32[4096]{0:T(1024)}), f32[2048]{0:T(1024)S(1)}, s32[]{:S(2)}) %slice-start.1) | async-done | bytes 8216 | tf_op jit(solution)/shard_map/slice | solution.py:155
  3.9 0.3 multiply_cosine_fusion.5
  4.2 0.3 multiply_cosine_fusion.8
  4.6 0.4 slice-done
  5.2 0.3 broadcast_select_fusion
  5.5 0.1 mul.1347
  5.7 0.1 mul.1353
  5.9 0.5 %multiply_cosine_fusion.7 = (f32[2,64,64]{2,1,0:T(8,128)S(1)}, f32[2,64,64]{2,1,0:T(8,128)S(1)}, f32[2,64,64]{2,1,0:T(8,128)S(1)}, f32[2,64,64]{2,1,0:T(8,128)S(1)}) fusion(f32[64]{0:T(128)S(1)} %squeeze_stack_reshape.16, f32[2,64]{1,0:T(2,128)S(1)} %neg.34, f32[64]{0:T(128)S(1)} %squeeze_stack_reshape.17), kind=kLoop, calls=%fused_computation.103 | loop fusion | flops 16384 | bytes 132096 | tf_op jit(solution)/shard_map/cos | solution.py:59
  6.6 1.0 %multiply_cosine_fusion.2 = (f32[256,64]{1,0:T(8,128)S(1)}, f32[256,64]{1,0:T(8,128)S(1)}, f32[256,64]{1,0:T(8,128)S(1)}, f32[256,64]{1,0:T(8,128)S(1)}) fusion(f32[64]{0:T(128)S(1)} %get-tuple-element.97, f32[256]{0:T(256)S(1)} %get-tuple-element.7, f32[64]{0:T(128)S(1)} %get-tuple-element.98), kind=kLoop, calls=%fused_computation.59 | loop fusion | flops 32768 | bytes 263680 | tf_op jit(solution)/shard_map/cos | solution.py:59
  7.6 0.2 multiply_subtract_fusion.9
  7.8 0.1 pad_maximum_fusion
  7.9 0.3 multiply_cosine_fusion.4
  8.2 0.3 multiply_cosine_fusion.11
  8.6 0.1 select_n.114
  8.7 0.1 select_n.117
  8.8 0.1 mul.1391
  8.9 0.1 mul.1392
  9.1 0.4 fusion.39
  9.5 0.2 multiply_subtract_fusion.8
  9.6 0.1 pad_maximum_fusion.1
  9.8 0.4 convolution_add_fusion
  10.1 0.1 fusion.38
  10.3 0.1 copy.42
  10.6 0.8 %copy.29 = f32[2,256,128]{2,0,1:T(2,128)} copy(f32[2,256,128]{1,2,0:T(8,128)S(1)} %maximum_multiply_fusion) | data formatting | bytes 524288 | tf_op jit(solution)/shard_map/mul | solution.py:124
  11.4 6.8 %all-to-all-start = ((f32[2,256,128]{2,0,1:T(2,128)}), f32[2,256,128]{2,0,1:T(2,128)S(1)}, u32[]{:S(2)}, u32[]{:S(2)}) async-start(f32[2,256,128]{2,0,1:T(2,128)} %copy.29), calls=%async_computation | async-start | bytes 524288 | tf_op jit(solution)/shard_map/all_to_all | solution.py:147
  18.2 0.2 multiply_cosine_fusion.9
  18.4 1.0 %multiply_cosine_fusion.1 = (f32[2,128,64]{2,1,0:T(8,128)S(1)}, f32[2,128,64]{2,1,0:T(8,128)S(1)}, f32[2,128,64]{2,1,0:T(8,128)S(1)}, f32[2,128,64]{2,1,0:T(8,128)S(1)}) fusion(f32[64]{0:T(128)S(1)} %mul.1317, f32[2,128]{1,0:T(2,128)S(1)} %neg.35, f32[64]{0:T(128)S(1)} %mul.1330), kind=kLoop, calls=%fused_computation.57 | loop fusion | flops 32768 | bytes 263680 | tf_op jit(solution)/shard_map/cos | solution.py:59
  19.4 8.4 %all-to-all-done = f32[2,256,128]{2,0,1:T(2,128)S(1)} async-done(((f32[2,256,128]{2,0,1:T(2,128)}), f32[2,256,128]{2,0,1:T(2,128)S(1)}, u32[]{:S(2)}, u32[]{:S(2)}) %all-to-all-start) | async-done | bytes 262176 | tf_op jit(solution)/shard_map/all_to_all | solution.py:147
  28.3 0.7 %fusion = f32[4,2,2,32,128]{4,3,2,1,0:T(8,128)S(1)} fusion(f32[4,2,2,32,64]{4,3,2,1,0:T(8,128)S(1)} %get-tuple-element.32, f32[4,2,2,32,64]{4,3,2,1,0:T(8,128)S(1)} %get-tuple-element.31, f32[4,2,2,32,64]{4,3,2,1,0:T(8,128)S(1)} %get-tuple-element.30, f32[4,2,2,32,64]{4,3,2,1,0:T(8,128)S(1)} %get-tuple-element.29, ...), kind=kOutput, calls=%fused_computation.2 | convolution fusion | flops 201719808 | bytes 917504 | tf_op jit(solution)/shard_map/dot_general | solution.py:72
  28.9 0.2 multiply_subtract_fusion.5
  29.1 0.4 fusion.22
  29.9 0.7 %fusion.8 = f32[2,2,2,64,128]{4,3,2,1,0:T(8,128)S(1)} fusion(f32[2,2,2,64,64]{4,3,2,1,0:T(8,128)S(1)} %get-tuple-element.24, f32[2,2,2,64,64]{4,3,2,1,0:T(8,128)S(1)} %get-tuple-element.23, f32[2,2,2,64,64]{4,3,2,1,0:T(8,128)S(1)} %get-tuple-element.22, f32[2,2,2,64,64]{4,3,2,1,0:T(8,128)S(1)} %get-tuple-element.21, f32[128,128]{1,0:T(8,128)S(1)} %mul.1392, ...), kind=kOutput, calls=%fused_computation.10 | convolution fusion | flops 201752576 | bytes 917504 | tf_op jit(solution)/shard_map/dot_general | solution.py:72
  30.6 0.2 multiply_subtract_fusion.2
  30.8 0.1 maximum_multiply_fusion.3
  31.1 0.1 multiply_subtract_fusion
  31.3 0.9 %convolution_bitcast_fusion = f32[1,2,2,128,128]{3,4,2,1,0:T(8,128)S(1)} fusion(f32[1,2,2,128,64]{4,3,2,1,0:T(8,128)S(1)} %get-tuple-element.12, f32[1,2,2,128,64]{4,3,2,1,0:T(8,128)S(1)} %get-tuple-element.11, f32[1,2,2,128,64]{4,3,2,1,0:T(8,128)S(1)} %get-tuple-element.104, f32[1,2,2,128,64]{4,3,2,1,0:T(8,128)S(1)} %get-tuple-element.105, ...), kind=kOutput, calls=%fused_computation | convolution fusion | flops 201719808 | bytes 917504 | tf_op jit(solution)/shard_map/dot_general | solution.py:72
  32.7 0.1 copy.35
  32.8 12.5 %all_to_all.20 = f32[2,256,128]{2,0,1:T(2,128)S(1)} all-to-all(f32[2,256,128]{2,0,1:T(2,128)S(1)} %copy.35), channel_id=1, replica_groups=mesh['shot'=2,'box'=8,'sub'=2] {'box'}, dimensions={1} | all-to-all | bytes 524288 | tf_op jit(solution)/shard_map/all_to_all | solution.py:165
  45.3 0.7 %copy.36 = f32[2,256,128]{2,1,0:T(8,128)} copy(f32[2,256,128]{2,0,1:T(2,128)S(1)} %all_to_all.20) | data formatting | bytes 524288 | tf_op jit(solution)/shard_map/all_to_all | solution.py:165
  (66 shorter events, 3.1 us)
Async XLA Ops:
  0.0 29.1 %copy-start = (f32[128,128]{1,0:T(8,128)S(1)}, f32[128,128]{1,0:T(8,128)}, u32[]{:S(2)}) copy-start(f32[128,128]{1,0:T(8,128)} %param.5) | copy-start | bytes 196612
  0.0 9.4 %collective-permute-start = (f32[2,256,128]{2,1,0:T(8,128)}, f32[2,256,128]{2,1,0:T(8,128)S(1)}, u32[]{:S(2)}, u32[]{:S(2)}) collective-permute-start(f32[2,256,128]{2,1,0:T(8,128)} %param.3), channel_id=1, source_target_pairs={{0,1},{1,0},{2,3},{3,2},{4,5},{5,4},{6,7},{7,6},{8,9},{9,8},{10,11... | collective-permute-start | bytes 786440 | tf_op jit(solution)/shard_map/ppermute | solution.py:13
  0.7 0.7 %copy-start.2 = (f32[4096]{0:T(1024)S(1)}, f32[4096]{0:T(1024)}, u32[]{:S(2)}) copy-start(f32[4096]{0:T(1024)} %param.4) | copy-start | bytes 49156
  3.0 0.7 %slice-start.1 = ((f32[4096]{0:T(1024)}), f32[2048]{0:T(1024)S(1)}, s32[]{:S(2)}) async-start(f32[4096]{0:T(1024)} %param.4), calls=%async_computation.3 | async-start | bytes 16384 | tf_op jit(solution)/shard_map/slice | solution.py:155
  4.2 0.7 %slice-start = ((f32[4096]{0:T(1024)}), f32[1024]{0:T(1024)S(1)}, s32[]{:S(2)}) async-start(f32[4096]{0:T(1024)} %param.4), calls=%async_computation.2 | async-start | bytes 8192 | tf_op jit(solution)/shard_map/slice | solution.py:155
  6.6 1.0 %copy-start.1 = (f32[2,256,128]{2,1,0:T(8,128)S(1)}, f32[2,256,128]{2,1,0:T(8,128)}, u32[]{:S(2)}) copy-start(f32[2,256,128]{2,1,0:T(8,128)} %param.3) | copy-start | bytes 786436
  11.4 16.4 %all-to-all-start = ((f32[2,256,128]{2,0,1:T(2,128)}), f32[2,256,128]{2,0,1:T(2,128)S(1)}, u32[]{:S(2)}, u32[]{:S(2)}) async-start(f32[2,256,128]{2,0,1:T(2,128)} %copy.29), calls=%async_computation | async-start | bytes 524288 | tf_op jit(solution)/shard_map/all_to_all | solution.py:147
where the time goes:
time: 46.4 us; the launch traced here: 46.1 us
  blocking collectives  12.5 us (27%)
  waiting for transfers between devices  8.38 us (18%)
  starting transfers between devices  7.3 us (16%)
  local copies, waits for them, and re-layouts  7.19 us (15%)
  other arithmetic  6.78 us (15%)
  matrix products  3.37 us (7%)
  between operations  0.55 us (1%)
    all_to_all x1, blocking collectives, body(): lax.all_to_all(spread, 'box', split_axis=1, concat_axis=1, tiled=True)  12.5 us
    all_to_all x1, waiting for transfers between devices, body(): lax.all_to_all(current, 'box', split_axis=1, concat_axis=0, tiled=True)  8.38 us
    all_to_all x1, starting transfers between devices, body(): lax.all_to_all(current, 'box', split_axis=1, concat_axis=0, tiled=True)  6.81 us
    cos x8, other arithmetic, rotate(): cosines = jnp.cos(angles)  3.91 us
    dot_general x3, matrix products, merge_blocks(): jnp.dot(joined.reshape(-1, 4 * CHEB * CHEB), weights, precision=lax.Preci...  2.23 us
    sub x11, other arithmetic, rotate(): real_part * cosines - imag_part * sine_vals  1.13 us
    unnamed x9, local copies, waits for them, and re-layouts  0.93 us
    slice x6, local copies, waits for them, and re-layouts, body(): velocity[:sub_count * groups * tgt_count]  0.93 us
  transfers between devices with their start and end apart: 2, of which 1 were waited for; matrix products, arithmetic and copies ran while one was open for 18% of the time, Pallas kernels for 0%

commit v1 on v0

--- a/solution.py
+++ b/solution.py
@@ -5,6 +5,22 @@
 
 CHEB = 8
 half_root = 0.7071067811865476
+
+
+def _save_results(unit, array_axis, original):
+    top = unit.shape
+    local_part = unit.reshape(
+        *top[:array_axis], original, top[array_axis] // original, *top[array_axis + 1 :]
+    )
+    field_out = jnp.moveaxis(local_part, array_axis, 0)
+    return field_out
+
+
+def attach_vectors(arr, axis_no):
+    val = list(arr.shape[1:])
+    val[axis_no] *= arr.shape[0]
+    ready = jnp.moveaxis(arr, 0, axis_no).reshape(val)
+    return ready
 
 
 def swapped(value, axis, apart):
@@ -162,7 +178,20 @@
         spread = merged.reshape(row_count // 2, 2 * col_count, vec_len)
         if level_idx == levels // 2 - 1:
             spread = apply_switch(spread, switch_kernel)
-    current = lax.all_to_all(spread, "box", split_axis=1, concat_axis=1, tiled=True)
+    t_next = jax.lax.axis_size("box")
+    v_now, plain = (t_next, jax.lax.axis_index("box"))
+    work_now = _save_results(spread, 1, v_now)
+    made = [work_now[plain]]
+    for hop_no in range(1, v_now):
+        h_now = work_now[(plain + hop_no) % v_now]
+        made.append(
+            jax.lax.ppermute(
+                h_now, axis_name="box", perm=[(s, (s + hop_no) % v_now) for s in range(v_now)]
+            )
+        )
+    piece_now = jnp.stack(made, axis=0)
+    work_now = piece_now[(plain - jnp.arange(v_now)) % v_now]
+    current = attach_vectors(work_now, 1)
     return current
 
 

time: 46.4 us -> 47.9 us (1.032)
  blocking collectives: 12.5 us -> 0 us
  starting transfers between devices: 7.3 us -> 17.8 us
  waiting for transfers between devices: 8.38 us -> 10.8 us
  other arithmetic: 6.78 us -> 8.63 us
  local copies, waits for them, and re-layouts: 7.19 us -> 6.22 us
    all_to_all x1 -> x0, blocking collectives: 12.5 us -> none  [body(): lax.all_to_all(spread, 'box', split_axis=1, concat_axis=1, tiled=True)]
    ppermute x0 -> x7, starting transfers between devices: none -> 10.5 us  [body(): jax.lax.ppermute(h_now, axis_name='box', perm=[(s, (s + hop_no) % v_now)...]
    ppermute x0 -> x7, waiting for transfers between devices: none -> 2.45 us  [body(): jax.lax.ppermute(h_now, axis_name='box', perm=[(s, (s + hop_no) % v_now)...]
    mul x1, other arithmetic: 0.03 us -> 1.06 us  [far_part(): rotate(mixture, omegas[None, :, None] * coord_out[None, None, :])]
    mul x1 -> x0, local copies, waits for them, and re-layouts: 0.84 us -> none  [far_part(): rotate(mixture, omegas[None, :, None] * coord_out[None, None, :])]
    transpose x0 -> x1, local copies, waits for them, and re-layouts: none -> 0.72 us  [attach_vectors(): ready = jnp.moveaxis(arr, 0, axis_no).reshape(val)]
    all_to_all x1 -> x0, local copies, waits for them, and re-layouts: 0.72 us -> none  [body(): lax.all_to_all(spread, 'box', split_axis=1, concat_axis=1, tiled=True)]
    gather x0 -> x1, local copies, waits for them, and re-layouts: none -> 0.56 us  [body(): work_now = piece_now[(plain - jnp.arange(v_now)) % v_now]]
  transfers between devices with their start and end apart: 2 -> 9, of which waited for: 1 -> 4; matrix products, arithmetic and copies ran while one was open for 18% -> 18% of each run, Pallas kernels for 0% -> 0%
where the time goes in v1:
time: 47.9 us; the launch traced here: 47.5 us
  starting transfers between devices  17.8 us (37%)
  waiting for transfers between devices  10.8 us (23%)
  other arithmetic  8.63 us (18%)
  local copies, waits for them, and re-layouts  6.22 us (13%)
  matrix products  3.37 us (7%)
  between operations  0.66 us (1%)
    ppermute x7, starting transfers between devices, body(): jax.lax.ppermute(h_now, axis_name='box', perm=[(s, (s + hop_no) % v_now)...  10.5 us
    all_to_all x1, waiting for transfers between devices, body(): lax.all_to_all(current, 'box', split_axis=1, concat_axis=0, tiled=True)  8.38 us
    all_to_all x1, starting transfers between devices, body(): lax.all_to_all(current, 'box', split_axis=1, concat_axis=0, tiled=True)  6.81 us
    cos x8, other arithmetic, rotate(): cosines = jnp.cos(angles)  4.14 us
    ppermute x7, waiting for transfers between devices, body(): jax.lax.ppermute(h_now, axis_name='box', perm=[(s, (s + hop_no) % v_now)...  2.45 us
    dot_general x3, matrix products, merge_blocks(): jnp.dot(joined.reshape(-1, 4 * CHEB * CHEB), weights, precision=lax.Preci...  2.22 us
    sub x11, other arithmetic, rotate(): real_part * cosines - imag_part * sine_vals  1.59 us
    mul x1, other arithmetic, far_part(): rotate(mixture, omegas[None, :, None] * coord_out[None, None, :])  1.06 us
  transfers between devices with their start and end apart: 9, of which 4 were waited for; matrix products, arithmetic and copies ran while one was open for 18% of the time, Pallas kernels for 0%

profile of v1, /device:TPU:0, one launch (start us, length us, event | category | flops | bytes accessed | tf_op | source)
XLA Modules:
  0.0 47.5 jit_solution(15765779093555726812)
XLA Ops:
  0.0 0.5 %collective-permute-start = (f32[2,256,128]{2,1,0:T(8,128)}, f32[2,256,128]{2,1,0:T(8,128)S(1)}, u32[]{:S(2)}, u32[]{:S(2)}) collective-permute-start(f32[2,256,128]{2,1,0:T(8,128)} %param.3), channel_id=1, source_target_pairs={{0,1},{1,0},{2,3},{3,2},{4,5},{5,4},{6,7},{7,6},{8,9},{9,8},{10,11... | collective-permute-start | bytes 786440 | tf_op jit(solution)/shard_map/ppermute | solution.py:29
  0.7 0.7 %copy-done.2 = f32[4096]{0:T(1024)S(1)} copy-done((f32[4096]{0:T(1024)S(1)}, f32[4096]{0:T(1024)}, u32[]{:S(2)}) %copy-start.2) | copy-done | bytes 16408
  1.8 0.2 select_reduce_fusion.2
  2.0 0.3 select_reduce_fusion.1
  2.4 0.1 broadcast_multiply_fusion
  3.2 0.5 %slice-done.1 = f32[2048]{0:T(1024)S(1)} async-done(((f32[4096]{0:T(1024)}), f32[2048]{0:T(1024)S(1)}, s32[]{:S(2)}) %slice-start.1) | async-done | bytes 8216 | tf_op jit(solution)/shard_map/slice | solution.py:171
  3.9 0.3 multiply_cosine_fusion.6
  4.3 0.5 %multiply_cosine_fusion.2 = (f32[256,64]{1,0:T(8,128)S(1)}, f32[256,64]{1,0:T(8,128)S(1)}) fusion(f32[64]{0:T(128)S(1)} %mul.1304, f32[256]{0:T(256)S(1)} %get-tuple-element.8), kind=kLoop, calls=%fused_computation.62 | loop fusion | flops 16384 | bytes 132352 | tf_op jit(solution)/shard_map/cos | solution.py:75
  4.8 0.1 slice-done
  5.2 0.3 broadcast_select_fusion
  5.5 0.1 mul.1349
  5.9 0.5 %multiply_cosine_fusion.8 = (f32[2,64,64]{2,1,0:T(8,128)S(1)}, f32[2,64,64]{2,1,0:T(8,128)S(1)}, f32[2,64,64]{2,1,0:T(8,128)S(1)}, f32[2,64,64]{2,1,0:T(8,128)S(1)}) fusion(f32[64]{0:T(128)S(1)} %squeeze_stack_reshape.16, f32[2,64]{1,0:T(2,128)S(1)} %neg.34, f32[64]{0:T(128)S(1)} %squeeze_stack_reshape.17), kind=kLoop, calls=%fused_computation.106 | loop fusion | flops 16384 | bytes 132096 | tf_op jit(solution)/shard_map/cos | solution.py:75
  6.6 1.0 %multiply_cosine_fusion.3 = (f32[256,64]{1,0:T(8,128)S(1)}, f32[256,64]{1,0:T(8,128)S(1)}, f32[256,64]{1,0:T(8,128)S(1)}, f32[256,64]{1,0:T(8,128)S(1)}) fusion(f32[64]{0:T(128)S(1)} %get-tuple-element.104, f32[256]{0:T(256)S(1)} %get-tuple-element.7, f32[64]{0:T(128)S(1)} %get-tuple-element.105), kind=kLoop, calls=%fused_computation.64 | loop fusion | flops 32768 | bytes 263680 | tf_op jit(solution)/shard_map/cos | solution.py:75
  7.6 0.2 multiply_subtract_fusion.10
  7.8 0.1 pad_maximum_fusion
  7.9 0.3 multiply_cosine_fusion.5
  8.2 0.3 multiply_cosine_fusion.11
  8.7 0.1 select_n.189
  9.2 0.4 fusion.42
  9.6 0.2 multiply_subtract_fusion.9
  9.8 0.1 pad_maximum_fusion.1
  9.9 0.4 convolution_add_fusion
  10.4 0.5 %multiply_subtract_fusion.8 = (f32[2,256,64]{2,0,1:T(2,128)S(1)}, f32[2,256,64]{2,0,1:T(2,128)S(1)}) fusion(f32[2,256,64]{2,1,0:T(8,128)S(1)} %get-tuple-element.47, f32[2,256,64]{2,1,0:T(8,128)S(1)} %get-tuple-element.46, f32[256,64]{1,0:T(8,128)S(1)} %get-tuple-element.89, f32[256,64]{1,0:T(8,128)S(1)} %get-tuple-element.88), kind=kLoop, calls=%fused_computation.52 | loop fusion | flops 196608 | bytes 655360 | tf_op jit(solution)/shard_map/sub | solution.py:78
  10.9 1.1 %maximum_multiply_fusion = f32[2,256,128]{2,0,1:T(2,128)} fusion(f32[2,256,64]{2,0,1:T(2,128)S(1)} %get-tuple-element.10, f32[2,256,64]{2,0,1:T(2,128)S(1)} %get-tuple-element.9), kind=kLoop, calls=%fused_computation.28 | loop fusion | flops 131072 | bytes 524288 | tf_op jit(solution)/shard_map/mul | solution.py:140
  12.0 6.8 %all-to-all-start = ((f32[2,256,128]{2,0,1:T(2,128)}), f32[2,256,128]{2,0,1:T(2,128)S(1)}, u32[]{:S(2)}, u32[]{:S(2)}) async-start(f32[2,256,128]{2,0,1:T(2,128)} %maximum_multiply_fusion), calls=%async_computation | async-start | bytes 524288 | tf_op jit(solution)/shard_map/all_to_all | solution.py:163
  18.8 0.2 multiply_cosine_fusion.9
  19.0 1.0 %multiply_cosine_fusion.1 = (f32[2,128,64]{2,1,0:T(8,128)S(1)}, f32[2,128,64]{2,1,0:T(8,128)S(1)}, f32[2,128,64]{2,1,0:T(8,128)S(1)}, f32[2,128,64]{2,1,0:T(8,128)S(1)}) fusion(f32[64]{0:T(128)S(1)} %mul.1319, f32[2,128]{1,0:T(2,128)S(1)} %neg.35, f32[64]{0:T(128)S(1)} %mul.1332), kind=kLoop, calls=%fused_computation.60 | loop fusion | flops 32768 | bytes 263680 | tf_op jit(solution)/shard_map/cos | solution.py:75
  20.0 8.4 %all-to-all-done = f32[2,256,128]{2,0,1:T(2,128)S(1)} async-done(((f32[2,256,128]{2,0,1:T(2,128)}), f32[2,256,128]{2,0,1:T(2,128)S(1)}, u32[]{:S(2)}, u32[]{:S(2)}) %all-to-all-start) | async-done | bytes 262176 | tf_op jit(solution)/shard_map/all_to_all | solution.py:163
  28.8 0.7 %fusion = f32[4,2,2,32,128]{4,3,2,1,0:T(8,128)S(1)} fusion(f32[4,2,2,32,64]{4,3,2,1,0:T(8,128)S(1)} %get-tuple-element.32, f32[4,2,2,32,64]{4,3,2,1,0:T(8,128)S(1)} %get-tuple-element.31, f32[4,2,2,32,64]{4,3,2,1,0:T(8,128)S(1)} %get-tuple-element.30, f32[4,2,2,32,64]{4,3,2,1,0:T(8,128)S(1)} %get-tuple-element.29, ...), kind=kOutput, calls=%fused_computation.3 | convolution fusion | flops 201719808 | bytes 917504 | tf_op jit(solution)/shard_map/dot_general | solution.py:88
  29.5 0.2 multiply_subtract_fusion.5
  29.6 0.4 fusion.22
  30.5 0.7 %fusion.8 = f32[2,2,2,64,128]{4,3,2,1,0:T(8,128)S(1)} fusion(f32[2,2,2,64,64]{4,3,2,1,0:T(8,128)S(1)} %get-tuple-element.26, f32[2,2,2,64,64]{4,3,2,1,0:T(8,128)S(1)} %get-tuple-element.25, f32[2,2,2,64,64]{4,3,2,1,0:T(8,128)S(1)} %get-tuple-element.24, f32[2,2,2,64,64]{4,3,2,1,0:T(8,128)S(1)} %get-tuple-element.23, f32[128,128]{1,0:T(8,128)S(1)} %mul.1394, ...), kind=kOutput, calls=%fused_computation.11 | convolution fusion | flops 201752576 | bytes 917504 | tf_op jit(solution)/shard_map/dot_general | solution.py:88
  31.1 0.2 multiply_subtract_fusion.2
  31.3 0.1 maximum_multiply_fusion.3
  31.7 0.1 multiply_subtract_fusion
  31.8 0.9 %convolution_bitcast_fusion = f32[1,2,2,128,128]{3,4,2,1,0:T(8,128)S(1)} fusion(f32[1,2,2,128,64]{4,3,2,1,0:T(8,128)S(1)} %get-tuple-element.14, f32[1,2,2,128,64]{4,3,2,1,0:T(8,128)S(1)} %get-tuple-element.13, f32[1,2,2,128,64]{4,3,2,1,0:T(8,128)S(1)} %get-tuple-element.111, f32[1,2,2,128,64]{4,3,2,1,0:T(8,128)S(1)} %get-tuple-element.112, ...), kind=kOutput, calls=%fused_computation.1 | convolution fusion | flops 201719808 | bytes 917504 | tf_op jit(solution)/shard_map/dot_general | solution.py:88
  33.0 0.1 maximum_multiply_fusion.4
  33.2 1.5 %collective-permute-start.1 = (f32[2,32,128]{2,1,0:T(8,128)S(1)}, f32[2,32,128]{2,1,0:T(8,128)S(1)}, u32[]{:S(2)}, u32[]{:S(2)}) collective-permute-start(f32[2,32,128]{2,1,0:T(8,128)S(1)} %get-tuple-element.39), channel_id=1, source_target_pairs={{0,2},{2,4},{4,6},{6,8},{8,10},{10,12},{12,14},{14,0},{1,3},{3,5},... | collective-permute-start | bytes 98312 | tf_op jit(solution)/shard_map/ppermute | solution.py:188
  34.7 1.7 %collective-permute-start.3 = (f32[2,32,128]{2,1,0:T(8,128)S(1)}, f32[2,32,128]{2,1,0:T(8,128)S(1)}, u32[]{:S(2)}, u32[]{:S(2)}) collective-permute-start(f32[2,32,128]{2,1,0:T(8,128)S(1)} %get-tuple-element.37), channel_id=1, source_target_pairs={{0,6},{2,8},{4,10},{6,12},{8,14},{10,0},{12,2},{14,4},{1,7},{3,9},... | collective-permute-start | bytes 98312 | tf_op jit(solution)/shard_map/ppermute | solution.py:188
  36.4 3.2 %collective-permute-start.4 = (f32[2,32,128]{2,1,0:T(8,128)S(1)}, f32[2,32,128]{2,1,0:T(8,128)S(1)}, u32[]{:S(2)}, u32[]{:S(2)}) collective-permute-start(f32[2,32,128]{2,1,0:T(8,128)S(1)} %get-tuple-element.36), channel_id=1, source_target_pairs={{0,8},{2,10},{4,12},{6,14},{8,0},{10,2},{12,4},{14,6},{1,9},{3,11}... | collective-permute-start | bytes 98312 | tf_op jit(solution)/shard_map/ppermute | solution.py:188
  39.6 0.9 %collective-permute-start.5 = (f32[2,32,128]{2,1,0:T(8,128)S(1)}, f32[2,32,128]{2,1,0:T(8,128)S(1)}, u32[]{:S(2)}, u32[]{:S(2)}) collective-permute-start(f32[2,32,128]{2,1,0:T(8,128)S(1)} %get-tuple-element.35), channel_id=1, source_target_pairs={{0,10},{2,12},{4,14},{6,0},{8,2},{10,4},{12,6},{14,8},{1,11},{3,13... | collective-permute-start | bytes 98312 | tf_op jit(solution)/shard_map/ppermute | solution.py:188
  40.5 1.8 %collective-permute-start.6 = (f32[2,32,128]{2,1,0:T(8,128)S(1)}, f32[2,32,128]{2,1,0:T(8,128)S(1)}, u32[]{:S(2)}, u32[]{:S(2)}) collective-permute-start(f32[2,32,128]{2,1,0:T(8,128)S(1)} %get-tuple-element.34), channel_id=1, source_target_pairs={{0,12},{2,14},{4,0},{6,2},{8,4},{10,6},{12,8},{14,10},{1,13},{3,15... | collective-permute-start | bytes 98312 | tf_op jit(solution)/shard_map/ppermute | solution.py:188
  42.3 1.4 %collective-permute-start.7 = (f32[2,32,128]{2,1,0:T(8,128)S(1)}, f32[2,32,128]{2,1,0:T(8,128)S(1)}, u32[]{:S(2)}, u32[]{:S(2)}) collective-permute-start(f32[2,32,128]{2,1,0:T(8,128)S(1)} %get-tuple-element.33), channel_id=1, source_target_pairs={{0,14},{2,0},{4,2},{6,4},{8,6},{10,8},{12,10},{14,12},{1,15},{3,1}... | collective-permute-start | bytes 98312 | tf_op jit(solution)/shard_map/ppermute | solution.py:188
  43.8 0.6 %collective-permute-done.5 = f32[2,32,128]{2,1,0:T(8,128)S(1)} collective-permute-done((f32[2,32,128]{2,1,0:T(8,128)S(1)}, f32[2,32,128]{2,1,0:T(8,128)S(1)}, u32[]{:S(2)}, u32[]{:S(2)}) %collective-permute-start.5) | collective-permute-done | bytes 32800 | tf_op jit(solution)/shard_map/ppermute | solution.py:188
  44.4 0.4 collective-permute-done.6
  44.8 1.5 %collective-permute-done.7 = f32[2,32,128]{2,1,0:T(8,128)S(1)} collective-permute-done((f32[2,32,128]{2,1,0:T(8,128)S(1)}, f32[2,32,128]{2,1,0:T(8,128)S(1)}, u32[]{:S(2)}, u32[]{:S(2)}) %collective-permute-start.7) | collective-permute-done | bytes 32800 | tf_op jit(solution)/shard_map/ppermute | solution.py:188
  46.3 0.6 %gather_fusion = f32[8,2,32,128]{3,2,1,0:T(8,128)S(1)} fusion(f32[8,2,32,128]{3,2,1,0:T(8,128)S(1)} %bitcast_dynamic-update-slice_fusion, s32[1024]{0:T(1024)S(1)} %pad_clamp_fusion), kind=kCustom, calls=%fused_computation | custom fusion | bytes 524320 | tf_op jit(solution)/shard_map/gather | solution.py:193
  46.8 0.7 %copy.28 = f32[2,8,32,128]{3,2,1,0:T(8,128)} copy(f32[2,8,32,128]{3,2,0,1:T(8,128)S(1)} %bitcast.126) | data formatting | bytes 524288 | tf_op jit(solution)/shard_map/transpose | solution.py:22
  (85 shorter events, 4.0 us)
Async XLA Ops:
  0.0 29.6 %copy-start = (f32[128,128]{1,0:T(8,128)S(1)}, f32[128,128]{1,0:T(8,128)}, u32[]{:S(2)}) copy-start(f32[128,128]{1,0:T(8,128)} %param.5) | copy-start | bytes 196612
  0.0 9.6 %collective-permute-start = (f32[2,256,128]{2,1,0:T(8,128)}, f32[2,256,128]{2,1,0:T(8,128)S(1)}, u32[]{:S(2)}, u32[]{:S(2)}) collective-permute-start(f32[2,256,128]{2,1,0:T(8,128)} %param.3), channel_id=1, source_target_pairs={{0,1},{1,0},{2,3},{3,2},{4,5},{5,4},{6,7},{7,6},{8,9},{9,8},{10,11... | collective-permute-start | bytes 786440 | tf_op jit(solution)/shard_map/ppermute | solution.py:29
  0.7 0.7 %copy-start.2 = (f32[4096]{0:T(1024)S(1)}, f32[4096]{0:T(1024)}, u32[]{:S(2)}) copy-start(f32[4096]{0:T(1024)} %param.4) | copy-start | bytes 49156
  3.0 0.7 %slice-start.1 = ((f32[4096]{0:T(1024)}), f32[2048]{0:T(1024)S(1)}, s32[]{:S(2)}) async-start(f32[4096]{0:T(1024)} %param.4), calls=%async_computation.2 | async-start | bytes 16384 | tf_op jit(solution)/shard_map/slice | solution.py:171
  4.2 0.7 %slice-start = ((f32[4096]{0:T(1024)}), f32[1024]{0:T(1024)S(1)}, s32[]{:S(2)}) async-start(f32[4096]{0:T(1024)} %param.4), calls=%async_computation.1 | async-start | bytes 8192 | tf_op jit(solution)/shard_map/slice | solution.py:171
  6.6 1.0 %copy-start.1 = (f32[2,256,128]{2,1,0:T(8,128)S(1)}, f32[2,256,128]{2,1,0:T(8,128)}, u32[]{:S(2)}) copy-start(f32[2,256,128]{2,1,0:T(8,128)} %param.3) | copy-start | bytes 786436
  12.0 16.4 %all-to-all-start = ((f32[2,256,128]{2,0,1:T(2,128)}), f32[2,256,128]{2,0,1:T(2,128)S(1)}, u32[]{:S(2)}, u32[]{:S(2)}) async-start(f32[2,256,128]{2,0,1:T(2,128)} %maximum_multiply_fusion), calls=%async_computation | async-start | bytes 524288 | tf_op jit(solution)/shard_map/all_to_all | solution.py:163
  33.2 7.3 %collective-permute-start.1 = (f32[2,32,128]{2,1,0:T(8,128)S(1)}, f32[2,32,128]{2,1,0:T(8,128)S(1)}, u32[]{:S(2)}, u32[]{:S(2)}) collective-permute-start(f32[2,32,128]{2,1,0:T(8,128)S(1)} %get-tuple-element.39), channel_id=1, source_target_pairs={{0,2},{2,4},{4,6},{6,8},{8,10},{10,12},{12,14},{14,0},{1,3},{3,5},... | collective-permute-start | bytes 98312 | tf_op jit(solution)/shard_map/ppermute | solution.py:188
  34.7 7.7 %collective-permute-start.2 = (f32[2,32,128]{2,1,0:T(8,128)S(1)}, f32[2,32,128]{2,1,0:T(8,128)S(1)}, u32[]{:S(2)}, u32[]{:S(2)}) collective-permute-start(f32[2,32,128]{2,1,0:T(8,128)S(1)} %get-tuple-element.38), channel_id=1, source_target_pairs={{0,4},{2,6},{4,8},{6,10},{8,12},{10,14},{12,0},{14,2},{1,5},{3,7},... | collective-permute-start | bytes 98312 | tf_op jit(solution)/shard_map/ppermute | solution.py:188
  34.7 9.0 %collective-permute-start.3 = (f32[2,32,128]{2,1,0:T(8,128)S(1)}, f32[2,32,128]{2,1,0:T(8,128)S(1)}, u32[]{:S(2)}, u32[]{:S(2)}) collective-permute-start(f32[2,32,128]{2,1,0:T(8,128)S(1)} %get-tuple-element.37), channel_id=1, source_target_pairs={{0,6},{2,8},{4,10},{6,12},{8,14},{10,0},{12,2},{14,4},{1,7},{3,9},... | collective-permute-start | bytes 98312 | tf_op jit(solution)/shard_map/ppermute | solution.py:188
  36.4 7.4 %collective-permute-start.4 = (f32[2,32,128]{2,1,0:T(8,128)S(1)}, f32[2,32,128]{2,1,0:T(8,128)S(1)}, u32[]{:S(2)}, u32[]{:S(2)}) collective-permute-start(f32[2,32,128]{2,1,0:T(8,128)S(1)} %get-tuple-element.36), channel_id=1, source_target_pairs={{0,8},{2,10},{4,12},{6,14},{8,0},{10,2},{12,4},{14,6},{1,9},{3,11}... | collective-permute-start | bytes 98312 | tf_op jit(solution)/shard_map/ppermute | solution.py:188
  39.6 4.8 %collective-permute-start.5 = (f32[2,32,128]{2,1,0:T(8,128)S(1)}, f32[2,32,128]{2,1,0:T(8,128)S(1)}, u32[]{:S(2)}, u32[]{:S(2)}) collective-permute-start(f32[2,32,128]{2,1,0:T(8,128)S(1)} %get-tuple-element.35), channel_id=1, source_target_pairs={{0,10},{2,12},{4,14},{6,0},{8,2},{10,4},{12,6},{14,8},{1,11},{3,13... | collective-permute-start | bytes 98312 | tf_op jit(solution)/shard_map/ppermute | solution.py:188
  40.5 4.3 %collective-permute-start.6 = (f32[2,32,128]{2,1,0:T(8,128)S(1)}, f32[2,32,128]{2,1,0:T(8,128)S(1)}, u32[]{:S(2)}, u32[]{:S(2)}) collective-permute-start(f32[2,32,128]{2,1,0:T(8,128)S(1)} %get-tuple-element.34), channel_id=1, source_target_pairs={{0,12},{2,14},{4,0},{6,2},{8,4},{10,6},{12,8},{14,10},{1,13},{3,15... | collective-permute-start | bytes 98312 | tf_op jit(solution)/shard_map/ppermute | solution.py:188
  42.3 3.9 %collective-permute-start.7 = (f32[2,32,128]{2,1,0:T(8,128)S(1)}, f32[2,32,128]{2,1,0:T(8,128)S(1)}, u32[]{:S(2)}, u32[]{:S(2)}) collective-permute-start(f32[2,32,128]{2,1,0:T(8,128)S(1)} %get-tuple-element.33), channel_id=1, source_target_pairs={{0,14},{2,0},{4,2},{6,4},{8,6},{10,8},{12,10},{14,12},{1,15},{3,1}... | collective-permute-start | bytes 98312 | tf_op jit(solution)/shard_map/ppermute | solution.py:188
